TPU v7x, 512 devices: a whole 4x4x16 slice. The times are simulated.
512 devices in a mesh: seq: 128 (over z, y, core), mp: 4 (over x).
Axes of the slice: x: 4, y: 4, z: 16, core: 2. Of those that a mesh axis runs over, the one named last changes fastest.
Arguments:
- queries: bfloat16 [8192, 2048], P('seq', 'mp'), may hold values from -14 to 14
- keys: bfloat16 [8192, 2048], P('seq', 'mp'), may hold values from -14 to 14
- values: bfloat16 [8192, 2048], P('seq', 'mp'), may hold values from -6 to 6
- stream: bfloat16 [8192, 2048], P('seq', 'mp'), may hold values from -6 to 6
- seg_lengths: int32 [64], replicated, may hold values from 1 to 256, 8192 in all
- gain: float32 [2048], replicated, may hold values from 0.5 to 1.5
- w_out: bfloat16 [2048, 2048], P('mp', 'seq'), may hold values from -0.125 to 0.125
- w_gate: bfloat16 [2048, 3072], P('seq', 'mp'), may hold values from -0.125 to 0.125
- w_up: bfloat16 [2048, 3072], P('seq', 'mp'), may hold values from -0.125 to 0.125
- w_down: bfloat16 [3072, 2048], P('mp', 'seq'), may hold values from -0.109375 to 0.109375
Outputs:
- mixed: bfloat16 [8192, 2048], P('seq', 'mp')
Inputs may be any that keep to these rules, and one draw needn't show every extreme that they name: `seg_lengths`: the segments of landmarks 0 to 63 follow one another and cover the document's 8192 tokens.
All inputs are finite; a program needn't handle non-finite values.
Results may differ from a plain program's by a relative error of at most 0.014.
Values may be sent and summed in bfloat16 or wider, within the bound.
No kernel may reach another device: no remote copies, remote signals or barrier semaphores. Data moves between devices by JAX's collectives and lax.ppermute only.
A program may use at most 64 MiB of HBM per device.

v0:
```python
import math
import jax
import jax.numpy as jnp
from jax import lax
from jax.sharding import PartitionSpec as P

PINV_ITERS = 6
HEAD = 128
HIGH_ACCURACY = lax.Precision.HIGHEST
EPS = 1e-05


def inverse_rounds(anchor_block):
    eye = jnp.eye(anchor_block.shape[-1], dtype=jnp.float32)
    col_most = jnp.max(jnp.sum(anchor_block, axis=1), axis=-1)
    row_most = jnp.max(jnp.sum(anchor_block, axis=2), axis=-1)
    approx = jnp.swapaxes(anchor_block, 1, 2) / (col_most * row_most)[:, None, None]
    for step in range(PINV_ITERS):
        prod = jnp.einsum("hij,hjk->hik", anchor_block, approx, precision=HIGH_ACCURACY)
        inner = 7.0 * eye - prod
        inner = 15.0 * eye - jnp.einsum("hij,hjk->hik", prod, inner, precision=HIGH_ACCURACY)
        inner = 13.0 * eye - jnp.einsum("hij,hjk->hik", prod, inner, precision=HIGH_ACCURACY)
        approx = 0.25 * jnp.einsum("hij,hjk->hik", approx, inner, precision=HIGH_ACCURACY)
    return approx


def on_device(queries, keys, values, stream, seg_lengths, gain, w_out, w_gate, w_up, w_down):
    tok = queries.shape[0]
    width = queries.shape[1]
    heads = width // HEAD
    marks = seg_lengths.shape[0]
    score_scale = 1.0 / math.sqrt(HEAD)
    ends = jnp.cumsum(seg_lengths)
    starts = ends - seg_lengths
    place = lax.axis_index("seq") * tok + jnp.arange(tok, dtype=jnp.int32)
    member = ((place[:, None] >= starts[None, :]) & (place[:, None] < ends[None, :])).astype(
        jnp.bfloat16
    )
    query_part = jnp.dot(member.T, queries, preferred_element_type=jnp.float32)
    key_part = jnp.dot(member.T, keys, preferred_element_type=jnp.float32)
    query_sum, key_sum = lax.psum((query_part, key_part), "seq")
    counts = seg_lengths.astype(jnp.float32)[:, None]
    query_anchors = (query_sum / counts).reshape(marks, heads, HEAD)
    key_anchors = (key_sum / counts).reshape(marks, heads, HEAD)
    query_slice = queries.astype(jnp.float32).reshape(tok, heads, HEAD)
    key_slice = keys.astype(jnp.float32).reshape(tok, heads, HEAD)
    value_slice = values.astype(jnp.float32).reshape(tok, heads, HEAD)
    nearby_scores = jax.nn.softmax(
        jnp.einsum("brc,xrc->rbx", query_slice, key_anchors, precision=HIGH_ACCURACY) * score_scale,
        axis=-1,
    )
    anchor_block = jax.nn.softmax(
        jnp.einsum("oqc,bqc->qob", query_anchors, key_anchors, precision=HIGH_ACCURACY)
        * score_scale,
        axis=-1,
    )
    distant_scores = (
        jnp.einsum("gvb,lvb->vgl", query_anchors, key_slice, precision=HIGH_ACCURACY) * score_scale
    )
    local_peak = jnp.max(distant_scores, axis=-1)
    peak = lax.pmax(local_peak, "seq")
    layer_weights = jnp.exp(distant_scores - peak[..., None])
    local_mass = jnp.sum(layer_weights, axis=-1)
    slice_sum = jnp.einsum("vqb,bvn->vqn", layer_weights, value_slice, precision=HIGH_ACCURACY)
    mass, weighted = lax.psum((local_mass, slice_sum), "seq")
    collected_rows = weighted / mass[..., None]
    token_mixer = jnp.einsum(
        "svy,syc->svc", inverse_rounds(anchor_block), collected_rows, precision=HIGH_ACCURACY
    )
    attn = (
        jnp.einsum("ljz,lzx->jlx", nearby_scores, token_mixer, precision=HIGH_ACCURACY)
        .reshape(tok, width)
        .astype(jnp.bfloat16)
    )
    full_out = lax.all_gather(w_out, "seq", axis=1, tiled=True)
    out_terms = jnp.dot(attn, full_out, preferred_element_type=jnp.float32)
    proj = lax.psum_scatter(
        out_terms.astype(jnp.bfloat16), "mp", scatter_dimension=1, tiled=True
    ).astype(jnp.float32)
    resid = (stream.astype(jnp.float32) + proj).astype(jnp.bfloat16)
    whole = lax.all_gather(resid, "mp", axis=1, tiled=True)
    whole32 = whole.astype(jnp.float32)
    meansq = jnp.mean(whole32 * whole32, axis=-1, keepdims=True)
    normed = (whole32 * lax.rsqrt(meansq + EPS) * gain[None, :]).astype(jnp.bfloat16)
    full_gate, full_up = (
        lax.all_gather(w_gate, "seq", axis=0, tiled=True),
        lax.all_gather(w_up, "seq", axis=0, tiled=True),
    )
    gate = jnp.dot(normed, full_gate, preferred_element_type=jnp.float32)
    upper = jnp.dot(normed, full_up, preferred_element_type=jnp.float32)
    hidden = (jax.nn.silu(gate) * upper).astype(jnp.bfloat16)
    full_down = lax.all_gather(w_down, "seq", axis=1, tiled=True)
    down_terms = jnp.dot(hidden, full_down, preferred_element_type=jnp.float32)
    ffn = lax.psum_scatter(
        down_terms.astype(jnp.bfloat16), "mp", scatter_dimension=1, tiled=True
    ).astype(jnp.float32)
    return (resid.astype(jnp.float32) + ffn).astype(jnp.bfloat16)


def solution(mesh):
    return jax.shard_map(
        on_device,
        mesh=mesh,
        in_specs=(
            P("seq", "mp"),
            P("seq", "mp"),
            P("seq", "mp"),
            P("seq", "mp"),
            P(),
            P(),
            P("mp", "seq"),
            P("seq", "mp"),
            P("seq", "mp"),
            P("mp", "seq"),
        ),
        out_specs=P("seq", "mp"),
        check_vma=False,
    )
```

profile of v0, /device:TPU:8, one launch (start us, length us, event | category | flops | bytes accessed | tf_op | source)
XLA Modules:
  0.0 1539.0 jit_solution(13063598890913038582)
XLA Ops:
  6.5 0.8 copy.40
  7.5 0.7 fusion.82
  8.3 1.8 fusion.60
  10.1 0.9 fusion.59
  11.0 323.3 %all-reduce.4.cloned.1.call-done = f32[64,512]{1,0:T(8,128)} async-done(((f32[64,512]{1,0:T(8,128)}), f32[64,512]{1,0:T(8,128)}) %all-reduce.4.cloned.1.call-update) | async-done | bytes 131088 | tf_op jit(solution)/shard_map/psum | solution.py:41
  334.4 1.2 fusion.83
  335.6 243.6 %pmax.7 = f32[4,64]{1,0:T(4,128)S(1)} all-reduce(f32[4,64]{1,0:T(4,128)S(1)} %get-tuple-element.11), channel_id=1, replica_groups=mesh['seq'=128,'mp'=4] {'seq'}, use_global_device_ids=true, to_apply=%region_10.11 | all-reduce | flops 256 | bytes 2048 | tf_op jit(solution)/shard_map/pmax | solution.py:61
  579.2 1.8 fusion.29
  581.1 0.7 all-gather.5.cloned.1.call-update
  581.9 246.9 %psum.31 = f32[4,64]{1,0:T(4,128)S(1)} all-reduce(f32[4,64]{1,0:T(4,128)S(1)} %fusion.28), channel_id=1, replica_groups=mesh['seq'=128,'mp'=4] {'seq'}, use_global_device_ids=true, to_apply=%region_13.14 | all-reduce | flops 256 | bytes 2048 | tf_op jit(solution)/shard_map/psum | solution.py:65
  828.7 78.3 %all-reduce.6.cloned.1.call-done = (f32[64,512]{1,0:T(8,128)}, f32[4,64,128]{2,1,0:T(8,128)}) async-done(((f32[64,512]{1,0:T(8,128)}, f32[4,64,128]{2,1,0:T(8,128)}), (f32[64,512]{1,0:T(8,128)}, f32[4,64,128]{2,1,0:T(8,128)})) %all-reduce.6.cloned.1.call-update) | async-done | bytes 262160 | tf_op jit(solution)/shard_map/psum | solution.py:41
  907.0 1.3 fusion.85
  908.4 1.4 fusion.84
  910.2 0.4 fusion.68
  910.6 0.3 convolution_subtract_fusion.11
  911.2 0.3 convolution_multiply_fusion.8
  911.5 0.4 fusion.77
  911.9 0.3 convolution_subtract_fusion.9
  912.2 0.3 convolution_subtract_fusion.8
  912.4 0.3 convolution_multiply_fusion.7
  912.9 0.4 fusion.75
  913.3 0.3 convolution_subtract_fusion.7
  914.1 0.4 fusion.73
  914.5 0.3 convolution_subtract_fusion.5
  915.0 0.3 convolution_multiply_fusion.5
  915.3 0.4 fusion.71
  915.7 0.3 convolution_subtract_fusion.3
  916.5 0.4 fusion.69
  916.9 0.3 convolution_subtract_fusion.1
  917.2 0.3 convolution_subtract_fusion
  917.4 0.3 convolution_multiply_fusion.3
  917.7 0.4 fusion.22
  918.1 0.4 fusion.2
  918.5 127.5 %all-gather.5.cloned.1.call-done = bf16[512,2048]{0,1:T(8,128)(2,1)} async-done(((bf16[512,16]{0,1:T(8,128)(2,1)}), bf16[512,2048]{0,1:T(8,128)(2,1)}) %all-gather.5.cloned.1.call-update) | async-done | bytes 2097168 | tf_op jit(solution)/shard_map/all_gather | solution.py:75
  1045.9 3.0 convolution_convert_fusion.1
  1049.1 0.5 all-gather.7.cloned.1.call-update
  1049.7 0.5 all-gather.11.cloned.1.call-update
  1050.2 0.7 all-gather.9.cloned.1.call-update
  1051.0 23.7 %reduce-scatter.3.cloned.1.call-done = bf16[64,512]{1,0:T(8,128)(2,1)} async-done(((bf16[64,2048]{1,0:T(8,128)(2,1)}), bf16[64,512]{1,0:T(8,128)(2,1)}) %reduce-scatter.3.cloned.1.call-update) | async-done | bytes 65552 | tf_op jit(solution)/shard_map/reduce_scatter | solution.py:77
  1074.6 0.9 add_convert_fusion.1
  1075.5 12.3 all_gather.16
  1087.9 130.2 %all-gather.7.cloned.1.call-done = bf16[2048,768]{1,0:T(8,128)(2,1)} async-done(((bf16[16,768]{1,0:T(8,128)(2,1)}), bf16[2048,768]{1,0:T(8,128)(2,1)}) %all-gather.7.cloned.1.call-update) | async-done | bytes 3145744 | tf_op jit(solution)/shard_map/all_gather | solution.py:86
  1218.1 2.6 fusion.36
  1220.7 138.2 %all-gather.11.cloned.1.call-done = bf16[768,2048]{0,1:T(8,128)(2,1)} async-done(((bf16[768,16]{0,1:T(8,128)(2,1)}), bf16[768,2048]{0,1:T(8,128)(2,1)}) %all-gather.11.cloned.1.call-update) | async-done | bytes 3145744 | tf_op jit(solution)/shard_map/all_gather | solution.py:92
  1358.9 140.9 %all-gather.9.cloned.1.call-done = bf16[2048,768]{1,0:T(8,128)(2,1)} async-done(((bf16[16,768]{1,0:T(8,128)(2,1)}), bf16[2048,768]{1,0:T(8,128)(2,1)}) %all-gather.9.cloned.1.call-update) | async-done | bytes 3145744 | tf_op jit(solution)/shard_map/all_gather | solution.py:87
  1499.8 5.3 convolution_convert_fusion
  1505.1 25.5 %reduce-scatter.5.cloned.1.call-done = bf16[64,512]{1,0:T(8,128)(2,1)} async-done(((bf16[64,2048]{1,0:T(8,128)(2,1)}), bf16[64,512]{1,0:T(8,128)(2,1)}) %reduce-scatter.5.cloned.1.call-update) | async-done | bytes 65552 | tf_op jit(solution)/shard_map/reduce_scatter | solution.py:94
  1530.6 1.5 add_convert_fusion
  (39 shorter events, 2.9 us)
Async XLA Ops:
  6.5 3.6 copy-start
  6.5 327.8 %all-reduce.4.cloned.1.call-start = ((), (), s32[]{:S(2)}) async-start(), calls=%async_computation.2 | async-start | bytes 262144 | tf_op jit(solution)/shard_map/psum | solution.py:41
  10.1 897.0 %all-reduce.6.cloned.1.call-start = ((), (), s32[]{:S(2)}) async-start(), calls=%async_computation.9 | async-start | bytes 524288 | tf_op jit(solution)/shard_map/psum | solution.py:41
  581.0 464.9 %all-gather.5.cloned.1.call-start = ((), (), s32[]{:S(2)}) async-start(), calls=%async_computation.3 | async-start | bytes 2113536 | tf_op jit(solution)/shard_map/all_gather | solution.py:75
  581.7 492.9 %reduce-scatter.3.cloned.1.call-start = ((), (), s32[]{:S(2)}) async-start(), calls=%async_computation.4 | async-start | bytes 327680 | tf_op jit(solution)/shard_map/reduce_scatter | solution.py:77
  913.6 4.2 copy-start.3
  916.0 158.7 %copy-start.1 = (bf16[64,512]{1,0:T(8,128)(2,1)S(1)}, bf16[64,512]{1,0:T(8,128)(2,1)}, u32[]{:S(2)}) copy-start(bf16[64,512]{1,0:T(8,128)(2,1)} %param.13) | copy-start | bytes 196612
  916.5 301.6 %copy-start.2 = (f32[2048]{0:T(1024)S(1)}, f32[2048]{0:T(1024)}, u32[]{:S(2)}) copy-start(f32[2048]{0:T(1024)} %param.15) | copy-start | bytes 24580
  1049.0 169.1 %all-gather.7.cloned.1.call-start = ((), (), s32[]{:S(2)}) async-start(), calls=%async_computation.5 | async-start | bytes 3170304 | tf_op jit(solution)/shard_map/all_gather | solution.py:86
  1049.6 309.3 %all-gather.11.cloned.1.call-start = ((), (), s32[]{:S(2)}) async-start(), calls=%async_computation.7 | async-start | bytes 3170304 | tf_op jit(solution)/shard_map/all_gather | solution.py:92
  1050.2 449.6 %all-gather.9.cloned.1.call-start = ((), (), s32[]{:S(2)}) async-start(), calls=%async_computation.6 | async-start | bytes 3170304 | tf_op jit(solution)/shard_map/all_gather | solution.py:87
  1050.9 479.7 %reduce-scatter.5.cloned.1.call-start = ((), (), s32[]{:S(2)}) async-start(), calls=%async_computation.8 | async-start | bytes 327680 | tf_op jit(solution)/shard_map/reduce_scatter | solution.py:94
Sparse Core Ops, SparseCore 0:
  10.8 323.5 all-reduce.3
  581.1 325.8 all-reduce.5
  910.2 135.7 all-gather.4
  1049.1 25.4 reduce-scatter.2
  1078.1 139.9 all-gather.6
  1221.6 137.2 all-gather.10
  1362.5 137.2 all-gather.8
  1505.2 25.3 reduce-scatter.4
where the time goes:
time: 1540 us
  waiting for transfers between devices  990 us (64%)
  blocking collectives  503 us (33%)
  matrix products  27.2 us (2%)
    psum x2, waiting for transfers between devices, on_device(): query_sum, key_sum = lax.psum((query_part, key_part), 'seq')  402 us
    psum x1, blocking collectives, on_device(): mass, weighted = lax.psum((local_mass, slice_sum), 'seq')  247 us
    pmax x1, blocking collectives, on_device(): peak = lax.pmax(local_peak, 'seq')  244 us
    all_gather x1, waiting for transfers between devices, on_device(): lax.all_gather(w_up, 'seq', axis=0, tiled=True)  141 us
    all_gather x1, waiting for transfers between devices, on_device(): full_down = lax.all_gather(w_down, 'seq', axis=1, tiled=True)  138 us
    all_gather x1, waiting for transfers between devices, on_device(): lax.all_gather(w_gate, 'seq', axis=0, tiled=True)  130 us
    all_gather x1, waiting for transfers between devices, on_device(): full_out = lax.all_gather(w_out, 'seq', axis=1, tiled=True)  127 us
  transfers between devices with their start and end apart: 8, of which 8 were waited for; matrix products, arithmetic and copies ran while one was open for 1% of the time, Pallas kernels for 0%

commit v1 on v0

--- a/solution.py
+++ b/solution.py
@@ -89,7 +89,9 @@
     gate = jnp.dot(normed, full_gate, preferred_element_type=jnp.float32)
     upper = jnp.dot(normed, full_up, preferred_element_type=jnp.float32)
     hidden = (jax.nn.silu(gate) * upper).astype(jnp.bfloat16)
-    full_down = lax.all_gather(w_down, "seq", axis=1, tiled=True)
+    full_down = jnp.concatenate(
+        lax.all_to_all(jnp.stack([w_down] * lax.axis_size("seq")), "seq", 0, 0), axis=1
+    )
     down_terms = jnp.dot(hidden, full_down, preferred_element_type=jnp.float32)
     ffn = lax.psum_scatter(
         down_terms.astype(jnp.bfloat16), "mp", scatter_dimension=1, tiled=True

time: 1540 us -> 1420 us (0.922)
  waiting for transfers between devices: 990 us -> 855 us
    all_gather x1 -> x0, waiting for transfers between devices: 138 us -> none  [on_device(): full_down = lax.all_gather(w_down, 'seq', axis=1, tiled=True)]
    all_gather x1, waiting for transfers between devices: 130 us -> 152 us  [on_device(): lax.all_gather(w_gate, 'seq', axis=0, tiled=True)]
  transfers between devices with their start and end apart: 8 -> 8, of which waited for: 8 -> 7; matrix products, arithmetic and copies ran while one was open for 1% -> 1% of each run, Pallas kernels for 0% -> 0%
where the time goes in v1:
time: 1420 us
  waiting for transfers between devices  855 us (60%)
  blocking collectives  503 us (35%)
  matrix products  27 us (2%)
    psum x2, waiting for transfers between devices, on_device(): query_sum, key_sum = lax.psum((query_part, key_part), 'seq')  402 us
    psum x1, blocking collectives, on_device(): mass, weighted = lax.psum((local_mass, slice_sum), 'seq')  247 us
    pmax x1, blocking collectives, on_device(): peak = lax.pmax(local_peak, 'seq')  244 us
    all_gather x1, waiting for transfers between devices, on_device(): lax.all_gather(w_gate, 'seq', axis=0, tiled=True)  152 us
    all_gather x1, waiting for transfers between devices, on_device(): lax.all_gather(w_up, 'seq', axis=0, tiled=True)  136 us
    all_gather x1, waiting for transfers between devices, on_device(): full_out = lax.all_gather(w_out, 'seq', axis=1, tiled=True)  127 us
  transfers between devices with their start and end apart: 8, of which 7 were waited for; matrix products, arithmetic and copies ran while one was open for 1% of the time, Pallas kernels for 0%

profile of v1, /device:TPU:8, one launch (start us, length us, event | category | flops | bytes accessed | tf_op | source)
XLA Modules:
  0.0 1418.1 jit_solution(9470087091315285443)
XLA Ops:
  6.5 0.8 copy.41
  7.5 0.7 fusion.82
  8.3 1.8 fusion.60
  10.1 0.9 fusion.59
  11.0 323.3 %all-reduce.4.cloned.1.call-done = f32[64,512]{1,0:T(8,128)} async-done(((f32[64,512]{1,0:T(8,128)}), f32[64,512]{1,0:T(8,128)}) %all-reduce.4.cloned.1.call-update) | async-done | bytes 131088 | tf_op jit(solution)/shard_map/psum | solution.py:41
  334.4 1.2 fusion.83
  335.6 243.6 %pmax.7 = f32[4,64]{1,0:T(4,128)S(1)} all-reduce(f32[4,64]{1,0:T(4,128)S(1)} %get-tuple-element.11), channel_id=1, replica_groups=mesh['seq'=128,'mp'=4] {'seq'}, use_global_device_ids=true, to_apply=%region_10.11 | all-reduce | flops 256 | bytes 2048 | tf_op jit(solution)/shard_map/pmax | solution.py:61
  579.2 1.8 fusion.29
  581.1 0.7 all-gather.4.cloned.1.call-update
  581.9 246.9 %psum.31 = f32[4,64]{1,0:T(4,128)S(1)} all-reduce(f32[4,64]{1,0:T(4,128)S(1)} %fusion.28), channel_id=1, replica_groups=mesh['seq'=128,'mp'=4] {'seq'}, use_global_device_ids=true, to_apply=%region_13.14 | all-reduce | flops 256 | bytes 2048 | tf_op jit(solution)/shard_map/psum | solution.py:65
  828.7 78.3 %all-reduce.6.cloned.1.call-done = (f32[64,512]{1,0:T(8,128)}, f32[4,64,128]{2,1,0:T(8,128)}) async-done(((f32[64,512]{1,0:T(8,128)}, f32[4,64,128]{2,1,0:T(8,128)}), (f32[64,512]{1,0:T(8,128)}, f32[4,64,128]{2,1,0:T(8,128)})) %all-reduce.6.cloned.1.call-update) | async-done | bytes 262160 | tf_op jit(solution)/shard_map/psum | solution.py:41
  907.0 1.3 fusion.85
  908.4 1.4 fusion.84
  910.2 0.4 fusion.68
  910.6 0.3 convolution_subtract_fusion.11
  911.2 0.3 convolution_multiply_fusion.8
  911.5 0.4 fusion.77
  911.9 0.3 convolution_subtract_fusion.9
  912.2 0.3 convolution_subtract_fusion.8
  912.4 0.3 convolution_multiply_fusion.7
  912.9 0.4 fusion.75
  913.3 0.3 convolution_subtract_fusion.7
  914.1 0.4 fusion.73
  914.5 0.3 convolution_subtract_fusion.5
  914.8 0.3 convolution_subtract_fusion.4
  915.0 0.3 convolution_multiply_fusion.5
  915.3 0.4 fusion.71
  915.7 0.3 convolution_subtract_fusion.3
  916.0 0.3 convolution_subtract_fusion.2
  916.5 0.4 fusion.69
  916.9 0.3 convolution_subtract_fusion.1
  917.7 0.4 fusion.22
  918.1 0.4 fusion.2
  918.4 127.5 %all-gather.4.cloned.1.call-done = bf16[512,2048]{0,1:T(8,128)(2,1)} async-done(((bf16[512,16]{0,1:T(8,128)(2,1)}), bf16[512,2048]{0,1:T(8,128)(2,1)}) %all-gather.4.cloned.1.call-update) | async-done | bytes 2097168 | tf_op jit(solution)/shard_map/all_gather | solution.py:75
  1045.9 3.0 convolution_convert_fusion.1
  1049.1 0.5 all-gather.6.cloned.1.call-update
  1049.6 1.9 stack.2
  1051.5 12.6 all-to-all-start
  1064.1 0.5 all-gather.8.cloned.1.call-update
  1064.7 9.9 reduce-scatter.3.cloned.1.call-done
  1074.6 0.9 add_convert_fusion.1
  1075.5 12.3 all_gather.13
  1087.9 152.4 %all-gather.6.cloned.1.call-done = bf16[2048,768]{1,0:T(8,128)(2,1)} async-done(((bf16[16,768]{1,0:T(8,128)(2,1)}), bf16[2048,768]{1,0:T(8,128)(2,1)}) %all-gather.6.cloned.1.call-update) | async-done | bytes 3145744 | tf_op jit(solution)/shard_map/all_gather | solution.py:86
  1240.3 3.3 fusion.36
  1243.6 136.2 %all-gather.8.cloned.1.call-done = bf16[2048,768]{1,0:T(8,128)(2,1)} async-done(((bf16[16,768]{1,0:T(8,128)(2,1)}), bf16[2048,768]{1,0:T(8,128)(2,1)}) %all-gather.8.cloned.1.call-update) | async-done | bytes 3145744 | tf_op jit(solution)/shard_map/all_gather | solution.py:87
  1379.8 4.4 convolution_convert_fusion
  1384.2 25.5 %reduce-scatter.5.cloned.1.call-done = bf16[64,512]{1,0:T(8,128)(2,1)} async-done(((bf16[64,2048]{1,0:T(8,128)(2,1)}), bf16[64,512]{1,0:T(8,128)(2,1)}) %reduce-scatter.5.cloned.1.call-update) | async-done | bytes 65552 | tf_op jit(solution)/shard_map/reduce_scatter | solution.py:96
  1409.8 1.5 add_convert_fusion
  (41 shorter events, 2.9 us)
Async XLA Ops:
  6.5 3.6 copy-start
  6.5 327.8 %all-reduce.4.cloned.1.call-start = ((), (), s32[]{:S(2)}) async-start(), calls=%async_computation.3 | async-start | bytes 262144 | tf_op jit(solution)/shard_map/psum | solution.py:41
  10.1 897.0 %all-reduce.6.cloned.1.call-start = ((), (), s32[]{:S(2)}) async-start(), calls=%async_computation.9 | async-start | bytes 524288 | tf_op jit(solution)/shard_map/psum | solution.py:41
  581.0 464.9 %all-gather.4.cloned.1.call-start = ((), (), s32[]{:S(2)}) async-start(), calls=%async_computation.4 | async-start | bytes 2113536 | tf_op jit(solution)/shard_map/all_gather | solution.py:75
  581.7 492.9 %reduce-scatter.3.cloned.1.call-start = ((), (), s32[]{:S(2)}) async-start(), calls=%async_computation.5 | async-start | bytes 327680 | tf_op jit(solution)/shard_map/reduce_scatter | solution.py:77
  913.6 4.2 copy-start.4
  916.0 133.6 %copy-start.3 = (bf16[768,16]{0,1:T(8,128)(2,1)S(1)}, bf16[768,16]{0,1:T(8,128)(2,1)}, u32[]{:S(2)}) copy-start(bf16[768,16]{0,1:T(8,128)(2,1)} %param.19) | copy-start | bytes 73732
  1049.0 191.3 %all-gather.6.cloned.1.call-start = ((), (), s32[]{:S(2)}) async-start(), calls=%async_computation.6 | async-start | bytes 3170304 | tf_op jit(solution)/shard_map/all_gather | solution.py:86
  1051.5 23.1 %copy-start.1 = (bf16[64,512]{1,0:T(8,128)(2,1)S(1)}, bf16[64,512]{1,0:T(8,128)(2,1)}, u32[]{:S(2)}) copy-start(bf16[64,512]{1,0:T(8,128)(2,1)} %param.13) | copy-start | bytes 196612
  1051.5 188.8 %copy-start.2 = (f32[2048]{0:T(1024)S(1)}, f32[2048]{0:T(1024)}, u32[]{:S(2)}) copy-start(f32[2048]{0:T(1024)} %param.15) | copy-start | bytes 24580
  1051.5 328.3 %all-to-all-start = ((bf16[128,768,16]{1,2,0:T(8,128)(2,1)}), bf16[128,768,16]{1,2,0:T(8,128)(2,1)S(1)}, u32[]{:S(2)}, u32[]{:S(2)}) async-start(bf16[128,768,16]{1,2,0:T(8,128)(2,1)} %stack.2), calls=%async_computation.1 | async-start | bytes 6291456 | tf_op jit(solution)/shard_map/all_to_all | solution.py:93
  1064.1 315.7 %all-gather.8.cloned.1.call-start = ((), (), s32[]{:S(2)}) async-start(), calls=%async_computation.7 | async-start | bytes 3170304 | tf_op jit(solution)/shard_map/all_gather | solution.py:87
  1064.7 345.1 %reduce-scatter.5.cloned.1.call-start = ((), (), s32[]{:S(2)}) async-start(), calls=%async_computation.8 | async-start | bytes 327680 | tf_op jit(solution)/shard_map/reduce_scatter | solution.py:96
Sparse Core Ops, SparseCore 0:
  10.8 323.5 all-reduce.3
  581.1 325.8 all-reduce.5
  910.2 135.7 all-gather.3
  1049.1 25.4 reduce-scatter.2
  1078.1 162.1 all-gather.5
  1243.8 135.9 all-gather.7
  1384.4 25.3 reduce-scatter.4
